TPU v7x, 32 devices: a whole 2x2x4 slice. The times are simulated.
32 devices in a mesh: pipe: 2 (over x), ep: 16 (over z, y, core).
Axes of the slice: x: 2, y: 2, z: 4, core: 2. Of those that a mesh axis runs over, the one named last changes fastest.
Arguments:
- fresh: bfloat16 [2, 1024, 3584], P(None, 'ep'), may hold values from -48 to 48
- pending: bfloat16 [1024, 3584], P('ep'), may hold values from -48 to 48
- expert_ids: int32 [2, 2, 1024, 8], P('pipe', None, 'ep'), may hold values from 0 to 15, as said below
- chosen_groups: int32 [2, 2, 1024, 4], P('pipe', None, 'ep'), may hold values from 0 to 7, as said below
- affinity: float32 [2, 2, 1024, 8], P('pipe', None, 'ep'), may hold values from 0.05 to 1
- norm_gain: float32 [2, 3584], P('pipe'), may hold values from 0.25 to 1.75
- w_gate_up: bfloat16 [2, 16, 3584, 2048], P('pipe', 'ep'), may hold values from -0.09375 to 0.09375
- w_down: bfloat16 [2, 16, 1024, 3584], P('pipe', 'ep'), may hold values from -0.1875 to 0.1875
Outputs:
- section_out: bfloat16 [2, 2, 1024, 3584], P('pipe', None, 'ep')
Inputs may be any that keep to these rules, and one draw needn't show every extreme that they name: `expert_ids`: each row names 8 different experts. Within one section and slot, the rows of one device (aligned blocks of 64 rows) name one expert at most 63 times, and in every such block some expert is named exactly 63 times. `chosen_groups`: each row names 4 different groups; expert e lies in group e // 2. A row's experts may lie outside its groups.
All inputs are finite; a program needn't handle non-finite values.
Results may differ from a plain program's by a relative error of at most 0.0052.
Values may be sent and summed in bfloat16 or wider, within the bound.
A program may use at most 128 MiB of HBM per device.

v0:
```python
import jax
import jax.numpy as jnp
from jax import lax
from jax.sharding import PartitionSpec as P

TOP = 8
GROUPS = 8


EPSILON = 1e-06
ROUTED_SCALE = 2.5


def from_behind(value, axis, steps):
    count = lax.axis_size(axis)
    first, last = (max(0, -steps), min(count, count - steps))
    return lax.ppermute(value, axis, [(source, source + steps) for source in range(first, last)])


def rms_scale(hidden, gain):
    widened = hidden.astype(jnp.float32)
    mean_square = jnp.mean(widened * widened, axis=-1, keepdims=True)
    return (widened * lax.rsqrt(mean_square + EPSILON) * gain).astype(jnp.bfloat16)


def gate_table(routes, groups, affinity, experts):
    per_group = experts // GROUPS
    owners = routes // per_group
    in_group = jnp.any(owners[:, :, None] == groups[:, None, :], axis=-1)
    summed = jnp.sum(affinity, axis=-1, keepdims=True)
    return ROUTED_SCALE * affinity * in_group.astype(jnp.float32) / summed


def slot_capacity(tokens, experts):
    spread = tokens * TOP * 5 // (4 * experts)
    needed = ((tokens - 1) * TOP + experts - TOP - 1) // (experts - TOP)
    return min(tokens, max(spread, needed))


def moe_layer(hidden, routes, groups, affinity, gain, w_gate_up, w_down):
    experts = lax.axis_size("ep")
    tokens = hidden.shape[0]
    capacity = slot_capacity(tokens, experts)
    normed = rms_scale(hidden, gain)
    weights = gate_table(routes, groups, affinity, experts)
    expert_iota = jnp.arange(experts, dtype=jnp.int32)
    matches = (routes[:, :, None] == expert_iota).astype(jnp.int32)
    per_token = jnp.sum(matches, axis=1)
    earlier = jnp.cumsum(per_token, axis=0) - per_token
    position = jnp.sum(matches * earlier[:, None, :], axis=-1)
    slot_index = routes * capacity + position
    slot_iota = jnp.arange(experts * capacity, dtype=jnp.int32)
    placing = jnp.any(slot_iota[:, None, None] == slot_index[None, :, :], axis=-1).astype(
        jnp.bfloat16
    )
    outgoing = jnp.dot(placing, normed, preferred_element_type=jnp.float32).astype(jnp.bfloat16)
    outgoing = outgoing.reshape(experts, capacity, normed.shape[1])
    hidden_units = w_down.shape[2]
    arrived_rows = lax.all_to_all(outgoing, "ep", split_axis=0, concat_axis=0, tiled=True)
    flat_rows = arrived_rows.reshape(-1, arrived_rows.shape[-1])
    joined = jnp.dot(flat_rows, w_gate_up[0, 0], preferred_element_type=jnp.float32)
    active = (jax.nn.silu(joined[:, :hidden_units]) * joined[:, hidden_units:]).astype(jnp.bfloat16)
    produced = jnp.dot(active, w_down[0, 0], preferred_element_type=jnp.float32).astype(
        jnp.bfloat16
    )
    returned = lax.all_to_all(
        produced.reshape(arrived_rows.shape), "ep", split_axis=0, concat_axis=0, tiled=True
    )
    gathered = jnp.take(returned.reshape(experts * capacity, -1), slot_index, axis=0)
    layer_out = hidden.astype(jnp.float32) + jnp.sum(
        weights[:, :, None] * gathered.astype(jnp.float32), axis=1
    )
    return layer_out.astype(jnp.bfloat16)


def per_device(fresh, pending, expert_ids, chosen_groups, affinity, norm_gain, w_gate_up, w_down):
    at_start = lax.axis_index("pipe") == 0

    def run_slot(place_index, layer_in):
        return moe_layer(
            layer_in,
            expert_ids[0, place_index],
            chosen_groups[0, place_index],
            affinity[0, place_index],
            norm_gain[0],
            w_gate_up,
            w_down,
        )

    first_out = run_slot(0, jnp.where(at_start, fresh[0], pending))
    handed = from_behind(first_out, "pipe", 1)
    second_out = run_slot(1, jnp.where(at_start, fresh[1], handed))
    return jnp.stack([first_out, second_out])[None]


def solution(mesh):
    return jax.shard_map(
        per_device,
        mesh=mesh,
        in_specs=(
            P(None, "ep", None),
            P("ep", None),
            P("pipe", None, "ep", None),
            P("pipe", None, "ep", None),
            P("pipe", None, "ep", None),
            P("pipe", None),
            P("pipe", "ep", None, None),
            P("pipe", "ep", None, None),
        ),
        out_specs=P("pipe", None, "ep", None),
        check_vma=False,
    )
```

profile of v0, /device:TPU:15, one launch (start us, length us, event | category | flops | bytes accessed | tf_op | source)
XLA Modules:
  0.0 844.1 jit_solution(15498248089259459397)
XLA Ops:
  10.1 6.1 reshape.191
  16.2 166.3 %all_to_all.20 = bf16[16,63,3584]{2,1,0:T(8,128)(2,1)} all-to-all(bf16[16,63,3584]{2,1,0:T(8,128)(2,1)} %reshape.191), channel_id=1, replica_groups=mesh['pipe'=2,'ep'=16] {'ep'}, dimensions={0} | all-to-all | bytes 14450688 | tf_op jit(solution)/shard_map/all_to_all | solution.py:59
  182.4 6.1 reshape.192
  188.5 19.8 %fusion.2 = f32[1008,2048]{1,0:T(8,128)S(1)} fusion(bf16[1008,3584]{1,0:T(8,128)(2,1)} %reshape.192, bf16[1,1,3584,2048]{3,2,1,0:T(8,128)(2,1)} %param.16), kind=kOutput, calls=%fused_computation.4 | convolution fusion | flops 14797504512 | bytes 30162944 | tf_op jit(solution)/shard_map/dot_general | solution.py:61
  208.3 12.8 %convolution_convert_fusion.3 = bf16[1008,3584]{1,0:T(8,128)(2,1)} fusion(bf16[1,1,1024,3584]{3,2,1,0:T(8,128)(2,1)} %param.17, f32[1008,2048]{1,0:T(8,128)S(1)} %fusion.2), kind=kOutput, calls=%fused_computation.9 | convolution fusion | flops 7408558080 | bytes 22822912 | tf_op jit(solution)/shard_map/dot_general | solution.py:63
  221.1 6.1 reshape.193
  227.2 6.0 all-to-all-start.1
  233.7 159.2 %all-to-all-done.1 = bf16[16,63,3584]{2,1,0:T(8,128)(2,1)} async-done(((bf16[16,63,3584]{2,1,0:T(8,128)(2,1)}), bf16[16,63,3584]{2,1,0:T(8,128)(2,1)}, u32[]{:S(2)}, u32[]{:S(2)}) %all-to-all-start.1) | async-done | bytes 7225376 | tf_op jit(solution)/shard_map/all_to_all | solution.py:66
  392.9 6.1 reshape.194
  399.1 11.9 %gather_fusion = bf16[512,3584]{1,0:T(8,128)(2,1)} fusion(bf16[1008,3584]{1,0:T(8,128)(2,1)} %reshape.194, s32[1024]{0:T(1024)S(1)} %pad_clamp_fusion.1), kind=kCustom, calls=%fused_computation.clone | custom fusion | bytes 7342080 | tf_op jit(solution)/shard_map/jit(_take)/gather | solution.py:69
  411.0 6.2 multiply_reduce_fusion.1
  419.6 11.5 %collective-permute-done = bf16[64,3584]{1,0:T(8,128)(2,1)S(1)} collective-permute-done((bf16[64,3584]{1,0:T(8,128)(2,1)S(1)}, bf16[64,3584]{1,0:T(8,128)(2,1)S(1)}, u32[]{:S(2)}, u32[]{:S(2)}) %collective-permute-start) | collective-permute-done | bytes 458784 | tf_op jit(solution)/shard_map/ppermute | solution.py:17
  431.4 5.1 convolution_convert_fusion
  436.5 6.1 reshape.195
  442.6 165.3 %all_to_all.21 = bf16[16,63,3584]{2,1,0:T(8,128)(2,1)} all-to-all(bf16[16,63,3584]{2,1,0:T(8,128)(2,1)} %reshape.195), channel_id=1, replica_groups=mesh['pipe'=2,'ep'=16] {'ep'}, dimensions={0} | all-to-all | bytes 14450688 | tf_op jit(solution)/shard_map/all_to_all | solution.py:59
  607.9 6.1 reshape.196
  614.0 19.8 %fusion = f32[1008,2048]{1,0:T(8,128)S(1)} fusion(bf16[1008,3584]{1,0:T(8,128)(2,1)} %reshape.196, bf16[1,1,3584,2048]{3,2,1,0:T(8,128)(2,1)} %param.16), kind=kOutput, calls=%fused_computation.2 | convolution fusion | flops 14797504512 | bytes 30162944 | tf_op jit(solution)/shard_map/dot_general | solution.py:61
  633.8 12.8 %convolution_convert_fusion.2 = bf16[1008,3584]{1,0:T(8,128)(2,1)} fusion(bf16[1,1,1024,3584]{3,2,1,0:T(8,128)(2,1)} %param.17, f32[1008,2048]{1,0:T(8,128)S(1)} %fusion), kind=kOutput, calls=%fused_computation.8 | convolution fusion | flops 7408558080 | bytes 22822912 | tf_op jit(solution)/shard_map/dot_general | solution.py:63
  646.6 6.1 reshape.197
  652.7 5.9 all-to-all-start.3
  659.0 159.4 %all-to-all-done.3 = bf16[16,63,3584]{2,1,0:T(8,128)(2,1)} async-done(((bf16[16,63,3584]{2,1,0:T(8,128)(2,1)}), bf16[16,63,3584]{2,1,0:T(8,128)(2,1)}, u32[]{:S(2)}, u32[]{:S(2)}) %all-to-all-start.3) | async-done | bytes 7225376 | tf_op jit(solution)/shard_map/all_to_all | solution.py:66
  818.4 6.1 reshape.198
  824.5 11.9 %gather_fusion.1 = bf16[512,3584]{1,0:T(8,128)(2,1)} fusion(bf16[1008,3584]{1,0:T(8,128)(2,1)} %reshape.198, s32[1024]{0:T(1024)S(1)} %pad_clamp_fusion), kind=kCustom, calls=%fused_computation.1.clone | custom fusion | bytes 7342080 | tf_op jit(solution)/shard_map/jit(_take)/gather | solution.py:69
  836.3 6.2 multiply_reduce_fusion
  (52 shorter events, 14.6 us)
Async XLA Ops:
  227.2 6.3 copy-start.2
  227.2 6.3 copy-start.3
  227.2 6.3 copy-start.1
  227.2 165.7 %all-to-all-start.1 = ((bf16[16,63,3584]{2,1,0:T(8,128)(2,1)}), bf16[16,63,3584]{2,1,0:T(8,128)(2,1)}, u32[]{:S(2)}, u32[]{:S(2)}) async-start(bf16[16,63,3584]{2,1,0:T(8,128)(2,1)} %reshape.193), calls=%async_computation.1 | async-start | bytes 14680064 | tf_op jit(solution)/shard_map/all_to_all | solution.py:66
  399.1 32.1 %copy-start = (bf16[2,64,3584]{2,1,0:T(8,128)(2,1)S(1)}, bf16[2,64,3584]{2,1,0:T(8,128)(2,1)}, u32[]{:S(2)}) copy-start(bf16[2,64,3584]{2,1,0:T(8,128)(2,1)} %param.10) | copy-start | bytes 2752516
  417.3 13.9 %collective-permute-start = (bf16[64,3584]{1,0:T(8,128)(2,1)S(1)}, bf16[64,3584]{1,0:T(8,128)(2,1)S(1)}, u32[]{:S(2)}, u32[]{:S(2)}) collective-permute-start(bf16[64,3584]{1,0:T(8,128)(2,1)S(1)} %fusion.17), channel_id=1, source_target_pairs={{0,16},{1,17},{2,18},{3,19},{4,20},{5,21},{6,22},{7,23},{8,24},{9,... | collective-permute-start | bytes 1376264 | tf_op jit(solution)/shard_map/ppermute | solution.py:17
  652.7 165.7 %all-to-all-start.3 = ((bf16[16,63,3584]{2,1,0:T(8,128)(2,1)}), bf16[16,63,3584]{2,1,0:T(8,128)(2,1)}, u32[]{:S(2)}, u32[]{:S(2)}) async-start(bf16[16,63,3584]{2,1,0:T(8,128)(2,1)} %reshape.197), calls=%async_computation.3 | async-start | bytes 14680064 | tf_op jit(solution)/shard_map/all_to_all | solution.py:66
where the time goes:
time: 852 us; the launch traced here: 844 us
  blocking collectives  332 us (39%)
  waiting for transfers between devices  330 us (39%)
  matrix products  75.3 us (9%)
  local copies, waits for them, and re-layouts  74.5 us (9%)
  other arithmetic  18.5 us (2%)
  starting transfers between devices  13.4 us (2%)
    all_to_all x2, blocking collectives, moe_layer(): lax.all_to_all(outgoing, 'ep', split_axis=0, concat_axis=0, tiled=True)  332 us
    all_to_all x2, waiting for transfers between devices, moe_layer(): lax.all_to_all(produced.reshape(arrived_rows.shape), 'ep', split_axis=0,...  319 us
    dot_general x2, matrix products, moe_layer(): jnp.dot(flat_rows, w_gate_up[0, 0], preferred_element_type=jnp.float32)  39.5 us
    dot_general x2, matrix products, moe_layer(): jnp.dot(active, w_down[0, 0], preferred_element_type=jnp.float32)  25.6 us
    gather x2, local copies, waits for them, and re-layouts, moe_layer(): jnp.take(returned.reshape(experts * capacity, -1), slot_index, axis=0)  23.8 us
  transfers between devices with their start and end apart: 3, of which 3 were waited for; matrix products, arithmetic and copies ran while one was open for 0% of the time, Pallas kernels for 0%

commit v1 on v0

--- a/solution.py
+++ b/solution.py
@@ -73,10 +73,46 @@
     return layer_out.astype(jnp.bfloat16)
 
 
+def gathers_whole_blocks(tokens, experts):
+    return 2 * slot_capacity(tokens, experts) > tokens
+
+
+def gate_columns(routes, groups, affinity, experts):
+    weights = gate_table(routes, groups, affinity, experts)
+    expert_iota = jnp.arange(experts, dtype=jnp.int32)
+    hit = routes[:, :, None] == expert_iota
+    return jnp.sum(jnp.where(hit, weights[:, :, None], 0.0), axis=1)
+
+
+def dense_layer(hidden, gates, gain, w_gate_up, w_down):
+    normed = rms_scale(hidden, gain)
+    hidden_units = w_down.shape[2]
+    rows = lax.all_gather(normed, "ep", axis=0, tiled=True)
+    joined = jnp.dot(rows, w_gate_up[0, 0], preferred_element_type=jnp.float32)
+    active = (jax.nn.silu(joined[:, :hidden_units]) * joined[:, hidden_units:]).astype(jnp.bfloat16)
+    produced = jnp.dot(active, w_down[0, 0], preferred_element_type=jnp.float32)
+    scaled = (produced * gates[:, None]).astype(jnp.bfloat16)
+    summed = lax.psum_scatter(scaled, "ep", scatter_dimension=0, tiled=True)
+    return (hidden.astype(jnp.float32) + summed.astype(jnp.float32)).astype(jnp.bfloat16)
+
+
 def per_device(fresh, pending, expert_ids, chosen_groups, affinity, norm_gain, w_gate_up, w_down):
     at_start = lax.axis_index("pipe") == 0
 
+    tokens, experts = pending.shape[0], lax.axis_size("ep")
+    gathering = gathers_whole_blocks(tokens, experts)
+    if gathering:
+        columns = jnp.stack(
+            [
+                gate_columns(expert_ids[0, j], chosen_groups[0, j], affinity[0, j], experts)
+                for j in range(2)
+            ]
+        )
+        columns = lax.all_to_all(columns, "ep", split_axis=2, concat_axis=1, tiled=True)[:, :, 0]
+
     def run_slot(place_index, layer_in):
+        if gathering:
+            return dense_layer(layer_in, columns[place_index], norm_gain[0], w_gate_up, w_down)
         return moe_layer(
             layer_in,
             expert_ids[0, place_index],

time: 852 us -> 420 us (0.49)
  blocking collectives: 332 us -> 10.6 us
  local copies, waits for them, and re-layouts: 74.5 us -> 2.37 us
  waiting for transfers between devices: 330 us -> 313 us
  between operations: 0.65 us -> 13.2 us
  starting transfers between devices: 13.4 us -> 1.42 us
  matrix products: 75.3 us -> 66 us
    all_to_all x2 -> x1, blocking collectives: 332 us -> 10.6 us  [per_device(): lax.all_to_all(columns, 'ep', split_axis=2, concat_axis=1, tiled=True)]
    all_to_all x2 -> x0, waiting for transfers between devices: 319 us -> none  [moe_layer(): lax.all_to_all(produced.reshape(arrived_rows.shape), 'ep', split_axis=0,...]
    reduce_scatter x0 -> x2, waiting for transfers between devices: none -> 181 us  [dense_layer(): summed = lax.psum_scatter(scaled, 'ep', scatter_dimension=0, tiled=True)]
    all_gather x0 -> x2, waiting for transfers between devices: none -> 121 us  [dense_layer(): rows = lax.all_gather(normed, 'ep', axis=0, tiled=True)]
    reshape x8 -> x0, local copies, waits for them, and re-layouts: 48.7 us -> none  [the longest x2 12.2 us: moe_layer(): produced.reshape(arrived_rows.shape)]
    gather x2 -> x0, local copies, waits for them, and re-layouts: 23.8 us -> none  [moe_layer(): jnp.take(returned.reshape(experts * capacity, -1), slot_index, axis=0)]
    reduce_sum x5 -> x2, other arithmetic: 12.5 us -> 0.03 us  [gate_columns(): return jnp.sum(jnp.where(hit, weights[:, :, None], 0.0), axis=1)]
    all_to_all x2 -> x0, starting transfers between devices: 11.9 us -> none  [moe_layer(): lax.all_to_all(produced.reshape(arrived_rows.shape), 'ep', split_axis=0,...]
  transfers between devices with their start and end apart: 3 -> 5, of which waited for: 3 -> 5; matrix products, arithmetic and copies ran while one was open for 0% -> 1% of each run, Pallas kernels for 0% -> 0%
where the time goes in v1:
time: 420 us; the launch traced here: 418 us
  waiting for transfers between devices  313 us (75%)
  matrix products  66 us (16%)
  between operations  13.2 us (3%)
  blocking collectives  10.6 us (3%)
  other arithmetic  10.5 us (2%)
    reduce_scatter x2, waiting for transfers between devices, dense_layer(): summed = lax.psum_scatter(scaled, 'ep', scatter_dimension=0, tiled=True)  181 us
    all_gather x2, waiting for transfers between devices, dense_layer(): rows = lax.all_gather(normed, 'ep', axis=0, tiled=True)  121 us
    dot_general x2, matrix products, dense_layer(): joined = jnp.dot(rows, w_gate_up[0, 0], preferred_element_type=jnp.float32)  40 us
    dot_general x2, matrix products, dense_layer(): produced = jnp.dot(active, w_down[0, 0], preferred_element_type=jnp.float32)  26 us
    ppermute x1, waiting for transfers between devices, from_behind(): lax.ppermute(value, axis, [(source, source + steps) for source in range(f...  11.3 us
    all_to_all x1, blocking collectives, per_device(): lax.all_to_all(columns, 'ep', split_axis=2, concat_axis=1, tiled=True)  10.6 us
  transfers between devices with their start and end apart: 5, of which 5 were waited for; matrix products, arithmetic and copies ran while one was open for 1% of the time, Pallas kernels for 0%

profile of v1, /device:TPU:15, one launch (start us, length us, event | category | flops | bytes accessed | tf_op | source)
XLA Modules:
  0.0 417.6 jit_solution(11396853199721783777)
XLA Ops:
  6.5 1.4 fusion.12
  8.0 0.8 reduce.2
  8.7 0.9 fusion.14
  9.8 0.7 slice_reduce_fusion.3
  10.5 0.7 slice_bitcast_fusion.3
  11.2 0.7 add_select_fusion.1
  11.9 0.7 slice_bitcast_fusion.1
  12.6 0.7 fusion.24
  13.5 10.6 %all_to_all.15 = f32[16,1,128]{2,1,0:T(1,128)S(1)} all-to-all(f32[16,1,128]{2,1,0:T(1,128)S(1)} %reshape.148), channel_id=1, replica_groups=mesh['pipe'=2,'ep'=16] {'ep'}, dimensions={0} | all-to-all | bytes 16384 | tf_op jit(solution)/shard_map/all_to_all | solution.py:111
  24.6 0.7 reduce.11
  25.6 52.7 %all-gather.3.cloned.1.call-done = bf16[1024,3584]{1,0:T(8,128)(2,1)} async-done(((bf16[64,3584]{1,0:T(8,128)(2,1)}), bf16[1024,3584]{1,0:T(8,128)(2,1)}) %all-gather.3.cloned.1.call-update) | async-done | bytes 7340048 | tf_op jit(solution)/shard_map/all_gather | solution.py:90
  78.2 20.0 %fusion.2 = f32[1024,2048]{1,0:T(8,128)S(1)} fusion(bf16[1024,3584]{1,0:T(8,128)(2,1)} %all-gather.3.cloned.1.call-done, bf16[1,1,3584,2048]{3,2,1,0:T(8,128)(2,1)} %param.14), kind=kOutput, calls=%fused_computation.2 | convolution fusion | flops 15032385536 | bytes 30408704 | tf_op jit(solution)/shard_map/dot_general | solution.py:91
  98.3 13.0 %multiply_convert_fusion.1 = bf16[1024,3584]{1,0:T(8,128)(2,1)} fusion(bf16[1,1,1024,3584]{3,2,1,0:T(8,128)(2,1)} %param.15, f32[1024]{0:T(1024)S(1)} %mul.111, f32[1024,2048]{1,0:T(8,128)S(1)} %fusion.2), kind=kOutput, calls=%fused_computation.5 | convolution fusion | flops 7529824256 | bytes 23072768 | tf_op jit(solution)/shard_map/dot_general | solution.py:93
  111.4 90.5 %reduce-scatter.3.cloned.1.call-done = bf16[64,3584]{1,0:T(8,128)(2,1)} async-done(((bf16[1024,3584]{1,0:T(8,128)(2,1)}), bf16[64,3584]{1,0:T(8,128)(2,1)}) %reduce-scatter.3.cloned.1.call-update) | async-done | bytes 458768 | tf_op jit(solution)/shard_map/reduce_scatter | solution.py:95
  201.8 1.1 fusion.15
  202.9 1.3 collective-permute-start
  204.2 11.3 %collective-permute-done = bf16[64,3584]{1,0:T(8,128)(2,1)S(1)} collective-permute-done((bf16[64,3584]{1,0:T(8,128)(2,1)S(1)}, bf16[64,3584]{1,0:T(8,128)(2,1)S(1)}, u32[]{:S(2)}, u32[]{:S(2)}) %collective-permute-start) | collective-permute-done | bytes 458784 | tf_op jit(solution)/shard_map/ppermute | solution.py:17
  215.9 1.0 fusion.18
  217.0 68.4 %all-gather.5.cloned.1.call-done = bf16[1024,3584]{1,0:T(8,128)(2,1)} async-done(((bf16[64,3584]{1,0:T(8,128)(2,1)}), bf16[1024,3584]{1,0:T(8,128)(2,1)}) %all-gather.5.cloned.1.call-update) | async-done | bytes 7340048 | tf_op jit(solution)/shard_map/all_gather | solution.py:90
  285.4 20.0 %fusion = f32[1024,2048]{1,0:T(8,128)S(1)} fusion(bf16[1024,3584]{1,0:T(8,128)(2,1)} %all-gather.5.cloned.1.call-done, bf16[1,1,3584,2048]{3,2,1,0:T(8,128)(2,1)} %param.14), kind=kOutput, calls=%fused_computation | convolution fusion | flops 15032385536 | bytes 30408704 | tf_op jit(solution)/shard_map/dot_general | solution.py:91
  305.4 13.0 %multiply_convert_fusion = bf16[1024,3584]{1,0:T(8,128)(2,1)} fusion(bf16[1,1,1024,3584]{3,2,1,0:T(8,128)(2,1)} %param.15, f32[1024]{0:T(1024)S(1)} %mul.120, f32[1024,2048]{1,0:T(8,128)S(1)} %fusion), kind=kOutput, calls=%fused_computation.4 | convolution fusion | flops 7529824256 | bytes 23072768 | tf_op jit(solution)/shard_map/dot_general | solution.py:93
  318.4 90.5 %reduce-scatter.5.cloned.1.call-done = bf16[64,3584]{1,0:T(8,128)(2,1)} async-done(((bf16[1024,3584]{1,0:T(8,128)(2,1)}), bf16[64,3584]{1,0:T(8,128)(2,1)}) %reduce-scatter.5.cloned.1.call-update) | async-done | bytes 458768 | tf_op jit(solution)/shard_map/reduce_scatter | solution.py:95
  408.9 1.1 fusion.20
  410.0 1.0 maximum_bitcast_fusion
  (25 shorter events, 1.5 us)
Async XLA Ops:
  6.5 71.7 %all-gather.3.cloned.1.call-start = ((), (), s32[]{:S(2)}) async-start(), calls=%async_computation.3 | async-start | bytes 7798784 | tf_op jit(solution)/shard_map/all_gather | solution.py:90
  9.7 192.1 %reduce-scatter.3.cloned.1.call-start = ((), (), s32[]{:S(2)}) async-start(), calls=%async_computation.4 | async-start | bytes 7798784 | tf_op jit(solution)/shard_map/reduce_scatter | solution.py:95
  111.3 104.3 %copy-start = (bf16[2,64,3584]{2,1,0:T(8,128)(2,1)S(1)}, bf16[2,64,3584]{2,1,0:T(8,128)(2,1)}, u32[]{:S(2)}) copy-start(bf16[2,64,3584]{2,1,0:T(8,128)(2,1)} %param.8) | copy-start | bytes 2752516
  111.3 174.1 %all-gather.5.cloned.1.call-start = ((), (), s32[]{:S(2)}) async-start(), calls=%async_computation.5 | async-start | bytes 7798784 | tf_op jit(solution)/shard_map/all_gather | solution.py:90
  202.9 12.6 %collective-permute-start = (bf16[64,3584]{1,0:T(8,128)(2,1)S(1)}, bf16[64,3584]{1,0:T(8,128)(2,1)S(1)}, u32[]{:S(2)}, u32[]{:S(2)}) collective-permute-start(bf16[64,3584]{1,0:T(8,128)(2,1)S(1)} %fusion.15), channel_id=1, source_target_pairs={{0,16},{1,17},{2,18},{3,19},{4,20},{5,21},{6,22},{7,23},{8,24},{9,... | collective-permute-start | bytes 1376264 | tf_op jit(solution)/shard_map/ppermute | solution.py:17
  216.8 192.1 %reduce-scatter.5.cloned.1.call-start = ((), (), s32[]{:S(2)}) async-start(), calls=%async_computation.6 | async-start | bytes 7798784 | tf_op jit(solution)/shard_map/reduce_scatter | solution.py:95
Sparse Core Ops, SparseCore 0:
  9.8 68.3 all-gather.2
  111.4 90.3 reduce-scatter.2
  217.0 68.3 all-gather.4
  318.5 90.3 reduce-scatter.4

commit v2 on v1

--- a/solution.py
+++ b/solution.py
@@ -1,6 +1,10 @@
+import functools
+
 import jax
 import jax.numpy as jnp
 from jax import lax
+from jax.experimental import pallas as pl
+from jax.experimental.pallas import tpu as pltpu
 from jax.sharding import PartitionSpec as P
 
 TOP = 8
@@ -74,7 +78,7 @@
 
 
 def gathers_whole_blocks(tokens, experts):
-    return 2 * slot_capacity(tokens, experts) > tokens
+    return experts % 4 == 0 and experts > 4 and 2 * slot_capacity(tokens, experts) > tokens
 
 
 def gate_columns(routes, groups, affinity, experts):
@@ -84,16 +88,218 @@
     return jnp.sum(jnp.where(hit, weights[:, :, None], 0.0), axis=1)
 
 
-def dense_layer(hidden, gates, gain, w_gate_up, w_down):
+def ring_place(device, chips):
+    chip = device // 2
+    z, y = chip // 2, chip % 2
+    return z + y * (chips - 1 - 2 * z)
+
+
+def ring_chip(place, chips):
+    y = place // (chips // 2)
+    z = place + y * (chips - 1 - 2 * place)
+    return 2 * z + y
+
+
+def ring_offsets(chips):
+    offsets = [0]
+    for step in range(1, chips // 2 + 1):
+        offsets.append(step)
+        if step < chips - step:
+            offsets.append(chips - step)
+    return offsets
+
+
+def ring_kernel(
+    chips, x_ref, h_ref, gate_ref, up_hbm, down_hbm, out_ref,
+    rows, part, act, from_twin, from_right, from_left, up, down,
+    load_sem, send_sem, recv_sem,
+):
+    tokens, width = x_ref.shape
+    hidden_units = down.shape[0]
+    ahead, behind = chips // 2, chips - 1 - chips // 2
+    offsets = ring_offsets(chips)
+    blocks = {offset: block for block, offset in enumerate(offsets)}
+
+    me = lax.axis_index("ep")
+    core = me % 2
+    place = ring_place(me, chips)
+    right = 2 * ring_chip((place + 1) % chips, chips) + core
+    left = 2 * ring_chip((place + chips - 1) % chips, chips) + core
+    twin = me + 1 - 2 * core
+
+    load_up = pltpu.make_async_copy(up_hbm.at[0, 0], up, load_sem.at[0])
+    load_down = pltpu.make_async_copy(down_hbm.at[0, 0], down, load_sem.at[1])
+    load_up.start()
+    load_down.start()
+
+    barrier = pltpu.get_barrier_semaphore()
+    for other in (left, right, twin):
+        pl.semaphore_signal(
+            barrier, inc=1, device_id={"ep": other}, device_id_type=pl.DeviceIdType.MESH
+        )
+    pl.semaphore_wait(barrier, 3)
+
+    copies = []
+
+    def send(source, target, other):
+        index = len(copies)
+        copy = pltpu.make_async_remote_copy(
+            src_ref=source,
+            dst_ref=target,
+            send_sem=send_sem.at[index],
+            recv_sem=recv_sem.at[index],
+            device_id={"ep": other},
+            device_id_type=pl.DeviceIdType.MESH,
+        )
+        copy.start()
+        copies.append(copy)
+        return copy
+
+    def mine(ref, block):
+        return ref.at[pl.ds(2 * block * tokens, tokens)]
+
+    def twins(ref, block):
+        return ref.at[pl.ds((2 * block + 1) * tokens, tokens)]
+
+    def one(ref, index):
+        return ref.at[pl.ds(index * tokens, tokens)]
+
+    def expert(block, count):
+        first, size = 2 * block * tokens, 2 * count * tokens
+        span = pl.ds(first, size)
+
+        @pl.loop(0, hidden_units // 256)
+        def _(tile):
+            at = pl.multiple_of(tile * 256, 256)
+            x = rows[span, :]
+            a = jnp.dot(x, up[:, pl.ds(at, 256)], preferred_element_type=jnp.float32)
+            b = jnp.dot(
+                x, up[:, pl.ds(hidden_units + at, 256)], preferred_element_type=jnp.float32
+            )
+            act[pl.ds(0, size), pl.ds(at, 256)] = (a / (1.0 + jnp.exp(-a)) * b).astype(act.dtype)
+
+        @pl.loop(0, width // 512)
+        def _(tile):
+            at = pl.multiple_of(tile * 512, 512)
+            y = jnp.dot(
+                act[pl.ds(0, size), :], down[:, pl.ds(at, 512)],
+                preferred_element_type=jnp.float32,
+            )
+            part[span, pl.ds(at, 512)] = (y * gate_ref[span, :]).astype(part.dtype)
+
+    def combine(block, *arrived):
+        at = pl.ds(2 * block * tokens, tokens)
+        total = part[at, :].astype(jnp.float32)
+        for ref, index in ((from_twin, block),) + arrived:
+            total += ref[pl.ds(index * tokens, tokens), :].astype(jnp.float32)
+        return total
+
+    def passed_on(block, *arrived):
+        part[pl.ds(2 * block * tokens, tokens), :] = combine(block, *arrived).astype(part.dtype)
+
+    gathers_right, gathers_left, forwards, swaps = {}, {}, {}, {}
+    gathers_right[1] = send(x_ref, mine(rows, blocks[1]), right)
+    gathers_left[1] = send(x_ref, mine(rows, blocks[chips - 1]), left)
+    forwards[0] = send(x_ref, twins(rows, 0), twin)
+    rows[pl.ds(0, tokens), :] = x_ref[...]
+    load_up.wait()
+    load_down.wait()
+
+    def swap(block):
+        swaps[block] = send(twins(part, block), one(from_twin, block), twin)
+
+    forwards[0].wait_recv()
+    expert(0, 1)
+    swap(0)
+    reduces_right, reduces_left = {}, {}
+    for step in range(1, ahead + 1):
+        group = [blocks[step]]
+        gathers_right[step].wait_recv()
+        if step < ahead:
+            gathers_right[step + 1] = send(
+                mine(rows, blocks[step]), mine(rows, blocks[step + 1]), right
+            )
+        forwards[blocks[step]] = send(
+            mine(rows, blocks[step]), twins(rows, blocks[step]), twin
+        )
+        if step <= behind:
+            here = blocks[chips - step]
+            group.append(here)
+            gathers_left[step].wait_recv()
+            if step < behind:
+                gathers_left[step + 1] = send(
+                    mine(rows, here), mine(rows, blocks[chips - step - 1]), left
+                )
+            forwards[here] = send(mine(rows, here), twins(rows, here), twin)
+        if step == behind + 1 and behind:
+            start = blocks[chips - behind]
+            swaps[start].wait_recv()
+            passed_on(start)
+            reduces_right[behind] = send(mine(part, start), one(from_left, behind - 1), right)
+        for block in group:
+            forwards[block].wait_recv()
+        expert(group[0], len(group))
+        for block in group:
+            swap(block)
+
+    start = blocks[ahead]
+    swaps[start].wait_recv()
+    passed_on(start)
+    reduces_left[ahead] = send(mine(part, start), one(from_right, ahead - 1), left)
+    for step in range(ahead - 1, 0, -1):
+        if step < behind:
+            here = blocks[chips - step]
+            swaps[here].wait_recv()
+            reduces_right[step + 1].wait_recv()
+            passed_on(here, (from_left, step))
+            reduces_right[step] = send(mine(part, here), one(from_left, step - 1), right)
+        here = blocks[step]
+        swaps[here].wait_recv()
+        reduces_left[step + 1].wait_recv()
+        passed_on(here, (from_right, step))
+        reduces_left[step] = send(mine(part, here), one(from_right, step - 1), left)
+    swaps[0].wait_recv()
+    reduces_right[1].wait_recv()
+    reduces_left[1].wait_recv()
+    total = combine(0, (from_left, 0), (from_right, 0))
+    out_ref[...] = (h_ref[...].astype(jnp.float32) + total).astype(out_ref.dtype)
+    for copy in copies:
+        copy.wait_send()
+
+
+def ring_layer(hidden, gates, gain, w_gate_up, w_down):
+    tokens, width = hidden.shape
+    experts = lax.axis_size("ep")
+    hidden_units = w_down.shape[2]
+    chips = experts // 2
+    ahead, behind = chips // 2, chips - 1 - chips // 2
+    exchanges = 2 * (ahead + behind) + 2 * chips
     normed = rms_scale(hidden, gain)
-    hidden_units = w_down.shape[2]
-    rows = lax.all_gather(normed, "ep", axis=0, tiled=True)
-    joined = jnp.dot(rows, w_gate_up[0, 0], preferred_element_type=jnp.float32)
-    active = (jax.nn.silu(joined[:, :hidden_units]) * joined[:, hidden_units:]).astype(jnp.bfloat16)
-    produced = jnp.dot(active, w_down[0, 0], preferred_element_type=jnp.float32)
-    scaled = (produced * gates[:, None]).astype(jnp.bfloat16)
-    summed = lax.psum_scatter(scaled, "ep", scatter_dimension=0, tiled=True)
-    return (hidden.astype(jnp.float32) + summed.astype(jnp.float32)).astype(jnp.bfloat16)
+    kind = hidden.dtype
+    in_vmem = pl.BlockSpec(memory_space=pltpu.VMEM)
+    in_hbm = pl.BlockSpec(memory_space=pl.ANY)
+    return pl.pallas_call(
+        functools.partial(ring_kernel, chips),
+        out_shape=jax.ShapeDtypeStruct((tokens, width), kind),
+        in_specs=[in_vmem, in_vmem, in_vmem, in_hbm, in_hbm],
+        out_specs=in_vmem,
+        scratch_shapes=[
+            pltpu.VMEM((experts * tokens, width), kind),
+            pltpu.VMEM((experts * tokens, width), kind),
+            pltpu.VMEM((4 * tokens, hidden_units), kind),
+            pltpu.VMEM((chips * tokens, width), kind),
+            pltpu.VMEM((ahead * tokens, width), kind),
+            pltpu.VMEM((behind * tokens, width), kind),
+            pltpu.VMEM(w_gate_up.shape[2:], kind),
+            pltpu.VMEM(w_down.shape[2:], kind),
+            pltpu.SemaphoreType.DMA((2,)),
+            pltpu.SemaphoreType.DMA((exchanges,)),
+            pltpu.SemaphoreType.DMA((exchanges,)),
+        ],
+        compiler_params=pltpu.CompilerParams(
+            collective_id=0, has_side_effects=True, vmem_limit_bytes=62_000_000
+        ),
+    )(normed, hidden, gates, w_gate_up, w_down)
 
 
 def per_device(fresh, pending, expert_ids, chosen_groups, affinity, norm_gain, w_gate_up, w_down):
@@ -109,10 +315,16 @@
             ]
         )
         columns = lax.all_to_all(columns, "ep", split_axis=2, concat_axis=1, tiled=True)[:, :, 0]
+        chips = experts // 2
+        me = lax.axis_index("ep")
+        places = (ring_place(me, chips) + chips - jnp.array(ring_offsets(chips))) % chips
+        order = 2 * ring_chip(places, chips)[:, None] + jnp.stack([me % 2, 1 - me % 2])
+        columns = jnp.take(columns.reshape(2, experts, tokens), order.reshape(-1), axis=1)
+        columns = columns.reshape(2, experts * tokens, 1)
 
     def run_slot(place_index, layer_in):
         if gathering:
-            return dense_layer(layer_in, columns[place_index], norm_gain[0], w_gate_up, w_down)
+            return ring_layer(layer_in, columns[place_index], norm_gain[0], w_gate_up, w_down)
         return moe_layer(
             layer_in,
             expert_ids[0, place_index],

time: 420 us -> 245 us (0.58)
  waiting for transfers between devices: 313 us -> 9.02 us
  Pallas kernels: 0 us -> 208 us
  matrix products: 66 us -> 0 us
  between operations: 13.2 us -> 0.15 us
  blocking collectives: 10.6 us -> 0 us
  starting transfers between devices: 1.42 us -> 8.13 us
    pallas_call x0 -> x2, Pallas kernels: none -> 208 us  [ring_layer(): pl.pallas_call(functools.partial(ring_kernel, chips), out_shape=jax.Shape...]
    reduce_scatter x2 -> x0, waiting for transfers between devices: 181 us -> none  [dense_layer(): summed = lax.psum_scatter(scaled, 'ep', scatter_dimension=0, tiled=True)]
    all_gather x2 -> x0, waiting for transfers between devices: 121 us -> none  [dense_layer(): rows = lax.all_gather(normed, 'ep', axis=0, tiled=True)]
    dot_general x4 -> x0, matrix products: 66 us -> none  [the longest x2 40 us: dense_layer(): joined = jnp.dot(rows, w_gate_up[0, 0], preferred_element_type=jnp.float32)]
    all_to_all x1 -> x0, blocking collectives: 10.6 us -> none  [per_device(): lax.all_to_all(columns, 'ep', split_axis=2, concat_axis=1, tiled=True)]
    all_to_all x0 -> x1, starting transfers between devices: none -> 6.52 us  [per_device(): lax.all_to_all(columns, 'ep', split_axis=2, concat_axis=1, tiled=True)]
  transfers between devices with their start and end apart: 5 -> 2, of which waited for: 5 -> 1; matrix products, arithmetic and copies ran while one was open for 1% -> 2% of each run, Pallas kernels for 0% -> 0%
where the time goes in v2:
time: 245 us; the launch traced here: 242 us
  Pallas kernels  208 us (85%)
  other arithmetic  10.3 us (4%)
  waiting for transfers between devices  9.02 us (4%)
  starting transfers between devices  8.13 us (3%)
  local copies, waits for them, and re-layouts  6.03 us (2%)
    pallas_call x2, Pallas kernels, ring_layer(): pl.pallas_call(functools.partial(ring_kernel, chips), out_shape=jax.Shape...  208 us
    ppermute x1, waiting for transfers between devices, from_behind(): lax.ppermute(value, axis, [(source, source + steps) for source in range(f...  9.02 us
    all_to_all x1, starting transfers between devices, per_device(): lax.all_to_all(columns, 'ep', split_axis=2, concat_axis=1, tiled=True)  6.52 us
  transfers between devices with their start and end apart: 2, of which 1 were waited for; matrix products, arithmetic and copies ran while one was open for 2% of the time, Pallas kernels for 0%

profile of v2, /device:TPU:15, one launch (start us, length us, event | category | flops | bytes accessed | tf_op | source)
XLA Modules:
  0.0 241.6 jit_solution(10863868773241465280)
XLA Ops:
  0.0 0.8 add_select_fusion.1
  0.8 0.7 slice_bitcast_fusion.1
  1.5 0.7 slice_bitcast_fusion.3
  2.2 0.7 slice_reduce_fusion.3
  2.9 0.7 fusion.9
  3.7 0.7 reshape.197
  4.4 6.5 %all-to-all-start = ((f32[16,1,128]{2,1,0:T(1,128)}), f32[16,1,128]{2,1,0:T(1,128)S(1)}, u32[]{:S(2)}, u32[]{:S(2)}) async-start(f32[16,1,128]{2,1,0:T(1,128)} %reshape.197), calls=%async_computation | async-start | bytes 16384 | tf_op jit(solution)/shard_map/all_to_all | solution.py:317
  10.9 0.7 add_multiply_fusion
  11.9 1.4 fusion
  13.4 0.8 reduce.2
  14.2 1.0 fusion.2.x_ref
  15.2 0.5 broadcast.241
  15.7 0.7 reduce.11
  16.4 0.6 gather_fusion
  17.0 0.1 select_bitcast_fusion
  17.2 1.3 squeeze.20.gate_ref
  18.4 101.5 %shard_map.91 = bf16[64,3584]{1,0:T(8,128)(2,1)} custom-call(bf16[64,3584]{1,0:T(8,128)(2,1)} %fusion.2.x_ref, bf16[64,3584]{1,0:T(8,128)(2,1)} %copy-done, f32[1024,1]{1,0:T(8,128)} %squeeze.20.gate_ref, bf16[1,1,3584,2048]{3,2,1,0:T(8,128)(2,1)} %up_hbm.3, bf16[1,1,1024,3584]{3,2,1,0:T(8,128)(2,1)} %down_hbm.3), custom_call_target="tpu_custom_call" | custom-call | tf_op jit(solution)/shard_map/pallas_call | solution.py:281
  120.0 1.6 collective-permute-start
  121.6 1.3 squeeze.21.gate_ref
  122.9 9.0 %collective-permute-done = bf16[64,3584]{1,0:T(8,128)(2,1)S(1)} collective-permute-done((bf16[64,3584]{1,0:T(8,128)(2,1)}, bf16[64,3584]{1,0:T(8,128)(2,1)S(1)}, u32[]{:S(2)}, u32[]{:S(2)}) %collective-permute-start) | collective-permute-done | bytes 458784 | tf_op jit(solution)/shard_map/ppermute | solution.py:21
  131.9 0.3 fusion.3
  132.2 1.0 fusion.5.x_ref
  133.1 106.5 %shard_map.92 = bf16[64,3584]{1,0:T(8,128)(2,1)} custom-call(bf16[64,3584]{1,0:T(8,128)(2,1)} %fusion.5.x_ref, bf16[64,3584]{1,0:T(8,128)(2,1)} %copy-done.1, f32[1024,1]{1,0:T(8,128)} %squeeze.21.gate_ref, bf16[1,1,3584,2048]{3,2,1,0:T(8,128)(2,1)} %up_hbm.3, bf16[1,1,1024,3584]{3,2,1,0:T(8,128)(2,1)} %down_hbm.3), custom_call_target="tpu_custom_call" | custom-call | tf_op jit(solution)/shard_map/pallas_call | solution.py:281
  239.6 2.0 maximum_bitcast_fusion
  (25 shorter events, 0.6 us)
Async XLA Ops:
  0.0 131.9 %copy-start.3 = (bf16[2,64,3584]{2,1,0:T(8,128)(2,1)S(1)}, bf16[2,64,3584]{2,1,0:T(8,128)(2,1)}, u32[]{:S(2)}) copy-start(bf16[2,64,3584]{2,1,0:T(8,128)(2,1)} %param.9) | copy-start | bytes 2752516
  4.4 10.8 %all-to-all-start = ((f32[16,1,128]{2,1,0:T(1,128)}), f32[16,1,128]{2,1,0:T(1,128)S(1)}, u32[]{:S(2)}, u32[]{:S(2)}) async-start(f32[16,1,128]{2,1,0:T(1,128)} %reshape.197), calls=%async_computation | async-start | bytes 16384 | tf_op jit(solution)/shard_map/all_to_all | solution.py:317
  13.4 5.1 %copy-start = (bf16[64,3584]{1,0:T(8,128)(2,1)}, bf16[64,3584]{1,0:T(8,128)(2,1)S(1)}, u32[]{:S(2)}) copy-start(bf16[64,3584]{1,0:T(8,128)(2,1)S(1)} %get-tuple-element.12.h_ref) | copy-start | bytes 1376260
  120.0 119.6 %copy-start.2 = (bf16[64,3584]{1,0:T(8,128)(2,1)S(1)}, bf16[64,3584]{1,0:T(8,128)(2,1)}, u32[]{:S(2)}) copy-start(bf16[64,3584]{1,0:T(8,128)(2,1)} %shard_map.91) | copy-start | bytes 1376260
  120.0 11.9 %collective-permute-start = (bf16[64,3584]{1,0:T(8,128)(2,1)}, bf16[64,3584]{1,0:T(8,128)(2,1)S(1)}, u32[]{:S(2)}, u32[]{:S(2)}) collective-permute-start(bf16[64,3584]{1,0:T(8,128)(2,1)} %shard_map.91), channel_id=1, source_target_pairs={{0,16},{1,17},{2,18},{3,19},{4,20},{5,21},{6,22},{7,23},{8,24},{9,... | collective-permute-start | bytes 1376264 | tf_op jit(solution)/shard_map/ppermute | solution.py:21
  132.2 1.0 copy-start.1

commit v3 on v1

--- a/solution.py
+++ b/solution.py
@@ -1,6 +1,10 @@
+import functools
+
 import jax
 import jax.numpy as jnp
 from jax import lax
+from jax.experimental import pallas as pl
+from jax.experimental.pallas import tpu as pltpu
 from jax.sharding import PartitionSpec as P
 
 TOP = 8
@@ -74,7 +78,8 @@
 
 
 def gathers_whole_blocks(tokens, experts):
-    return 2 * slot_capacity(tokens, experts) > tokens
+    ring = experts % 4 == 0 and experts > 8 and tokens % 32 == 0
+    return ring and 2 * slot_capacity(tokens, experts) > tokens
 
 
 def gate_columns(routes, groups, affinity, experts):
@@ -84,24 +89,295 @@
     return jnp.sum(jnp.where(hit, weights[:, :, None], 0.0), axis=1)
 
 
-def dense_layer(hidden, gates, gain, w_gate_up, w_down):
-    normed = rms_scale(hidden, gain)
+def ring_place(device, chips):
+    chip = device // 2
+    z, y = chip // 2, chip % 2
+    return z + y * (chips - 1 - 2 * z)
+
+
+def ring_chip(place, chips):
+    y = place // (chips // 2)
+    z = place + y * (chips - 1 - 2 * place)
+    return 2 * z + y
+
+
+def ring_offsets(chips):
+    offsets = [0]
+    for step in range(1, chips // 2 + 1):
+        offsets.append(step)
+        if step < chips - step:
+            offsets.append(chips - step)
+    return offsets
+
+
+def ring_kernel(
+    chips, first_ref, second_ref, gain_ref, gate_ref, up_hbm, down_hbm, out_ref,
+    rows, part, act, from_twin, from_right, from_left, held, up, down,
+    load_sem, send_sem, recv_sem, pipe_send_sem, pipe_recv_sem, done_sem,
+):
+    tokens, width = first_ref.shape
+    half_rows = tokens // 2
+    hidden_units = down.shape[0]
+    ahead = chips // 2
+    blocks = {offset: block for block, offset in enumerate(ring_offsets(chips))}
+
+    me, pipe = lax.axis_index("ep"), lax.axis_index("pipe")
+    core = me % 2
+    place = ring_place(me, chips)
+    right = 2 * ring_chip((place + 1) % chips, chips) + core
+    left = 2 * ring_chip((place + chips - 1) % chips, chips) + core
+    twin = me + 1 - 2 * core
+    MESH = pl.DeviceIdType.MESH
+
+    load_up = pltpu.make_async_copy(up_hbm.at[0, 0], up, load_sem.at[0])
+    load_down = pltpu.make_async_copy(down_hbm.at[0, 0], down, load_sem.at[1])
+    load_up.start()
+    load_down.start()
+
+    barrier = pltpu.get_barrier_semaphore()
+    for other in (left, right, twin):
+        pl.semaphore_signal(barrier, inc=1, device_id={"ep": other}, device_id_type=MESH)
+    pl.semaphore_signal(barrier, inc=1, device_id={"pipe": 1 - pipe}, device_id_type=MESH)
+    pl.semaphore_wait(barrier, 4)
+
+    def piece(ref, start, half):
+        return ref.at[pl.ds(start + half * half_rows, half_rows)]
+
+    def mine(ref, block, half):
+        return piece(ref, 2 * block * tokens, half)
+
+    def twins(ref, block, half):
+        return piece(ref, (2 * block + 1) * tokens, half)
+
+    def behind_of(step, toward):
+        return blocks[step if toward == "right" else chips - step]
+
+    def moves(step, half, toward):
+        lead = 0 if toward == "right" else 1
+        return step < ahead or (step == ahead and half == lead)
+
+    def expert_up(block, count):
+        span, size = pl.ds(2 * block * tokens, 2 * count * tokens), 2 * count * tokens
+
+        @pl.loop(0, hidden_units // 256)
+        def _(tile):
+            at = pl.multiple_of(tile * 256, 256)
+            x = rows[span, :]
+            a = jnp.dot(x, up[:, pl.ds(at, 256)], preferred_element_type=jnp.float32)
+            b = jnp.dot(
+                x, up[:, pl.ds(hidden_units + at, 256)], preferred_element_type=jnp.float32
+            )
+            act[pl.ds(0, size), pl.ds(at, 256)] = (a / (1.0 + jnp.exp(-a)) * b).astype(act.dtype)
+
+    def expert_down(slot, block, count):
+        span, size = pl.ds(2 * block * tokens, 2 * count * tokens), 2 * count * tokens
+
+        @pl.loop(0, width // 512)
+        def _(tile):
+            at = pl.multiple_of(tile * 512, 512)
+            y = jnp.dot(
+                act[pl.ds(0, size), :], down[:, pl.ds(at, 512)],
+                preferred_element_type=jnp.float32,
+            )
+            part[span, pl.ds(at, 512)] = (y * gate_ref[slot, span, :]).astype(part.dtype)
+
+    def combine(block, half, *arrived):
+        at = pl.ds(2 * block * tokens + half * half_rows, half_rows)
+        total = part[at, :].astype(jnp.float32)
+        for ref, index in ((from_twin, block),) + arrived:
+            span = pl.ds(index * tokens + half * half_rows, half_rows)
+            total += ref[span, :].astype(jnp.float32)
+        return total
+
+    def hand_on(half):
+        return pltpu.make_async_remote_copy(
+            src_ref=piece(out_ref.at[0], 0, half),
+            dst_ref=piece(held, 0, half),
+            send_sem=pipe_send_sem.at[half],
+            recv_sem=pipe_recv_sem.at[half],
+            device_id={"pipe": 1 - pipe},
+            device_id_type=MESH,
+        )
+
+    for slot in range(2):
+        copies = []
+
+        def send(source, target, other):
+            index = len(copies)
+            copy = pltpu.make_async_remote_copy(
+                src_ref=source,
+                dst_ref=target,
+                send_sem=send_sem.at[index],
+                recv_sem=recv_sem.at[index],
+                device_id={"ep": other},
+                device_id_type=MESH,
+            )
+            copy.start()
+            copies.append(copy)
+            return copy
+
+        gathers, forwards, swaps, reduces = {}, {}, {}, {}
+        layer_in = held if slot else first_ref
+        for half in range(2):
+            at = pl.ds(half * half_rows, half_rows)
+            if slot:
+
+                @pl.when(pipe == 0)
+                def _():
+                    held[at, :] = second_ref[at, :]
+
+                @pl.when(pipe == 1)
+                def _():
+                    hand_on(half).wait_recv()
+
+            widened = layer_in[at, :].astype(jnp.float32)
+            mean_square = jnp.mean(widened * widened, axis=-1, keepdims=True)
+            normed = widened * lax.rsqrt(mean_square + EPSILON) * gain_ref[...]
+            rows[at, :] = normed.astype(rows.dtype)
+            source = mine(rows, 0, half)
+            for toward, other in (("right", right), ("left", left)):
+                target = mine(rows, behind_of(1, toward), half)
+                gathers[1, half, toward] = send(source, target, other)
+            forwards[0, half] = send(source, twins(rows, 0, half), twin)
+
+        def arrive(step, half):
+            for toward, other in (("right", right), ("left", left)):
+                if not moves(step, half, toward):
+                    continue
+                here = behind_of(step, toward)
+                gathers[step, half, toward].wait_recv()
+                if moves(step + 1, half, toward):
+                    target = mine(rows, behind_of(step + 1, toward), half)
+                    gathers[step + 1, half, toward] = send(mine(rows, here, half), target, other)
+                forwards[here, half] = send(
+                    mine(rows, here, half), twins(rows, here, half), twin
+                )
+
+        def swap(block):
+            at = pl.ds((2 * block + 1) * tokens, tokens)
+            swaps[block] = send(
+                part.at[at], from_twin.at[pl.ds(block * tokens, tokens)], twin
+            )
+
+        swapped = set()
+
+        def reduce(step, half, toward):
+            here = behind_of(step, "left" if toward == "right" else "right")
+            if here not in swapped:
+                swaps[here].wait_recv()
+                swapped.add(here)
+            source, other = (from_left, right) if toward == "right" else (from_right, left)
+            arrived = ()
+            if moves(step + 1, half, toward):
+                reduces[step + 1, half, toward].wait_recv()
+                arrived = ((source, step),)
+            total = combine(here, half, *arrived)
+            at = pl.ds(2 * here * tokens + half * half_rows, half_rows)
+            part[at, :] = total.astype(part.dtype)
+            target = piece(source, (step - 1) * tokens, half)
+            reduces[step, half, toward] = send(mine(part, here, half), target, other)
+
+        group = [0]
+        if slot == 0:
+            load_up.wait()
+        for step in range(1, ahead + 1):
+            for block in group:
+                for half in range(2):
+                    forwards[block, half].wait_recv()
+            expert_up(group[0], len(group))
+            arrive(step, 0)
+            if step == ahead:
+                arrive(step, 1)
+            if slot == 0 and step == 1:
+                load_down.wait()
+            expert_down(slot, group[0], len(group))
+            for block in group:
+                swap(block)
+            if step < ahead:
+                arrive(step, 1)
+            group = [blocks[step]] + ([blocks[chips - step]] if 2 * step < chips else [])
+        reduce(ahead - 1, 1, "right")
+        reduce(ahead - 1, 0, "left")
+        for half in range(2):
+            forwards[group[0], half].wait_recv()
+        expert_up(group[0], 1)
+        expert_down(slot, group[0], 1)
+        swap(group[0])
+        for step in range(ahead, 0, -1):
+            reduce(step, 0, "right")
+            reduce(step, 1, "left")
+            if step > 2:
+                reduce(step - 2, 1, "right")
+                reduce(step - 2, 0, "left")
+        swaps[0].wait_recv()
+        for half in range(2):
+            reduces[1, half, "right"].wait_recv()
+            reduces[1, half, "left"].wait_recv()
+            at = pl.ds(half * half_rows, half_rows)
+            total = combine(0, half, (from_left, 0), (from_right, 0))
+            result = layer_in[at, :].astype(jnp.float32) + total
+            out_ref[slot, at, :] = result.astype(out_ref.dtype)
+            if slot == 0:
+
+                @pl.when(pipe == 0)
+                def _():
+                    hand_on(half).start()
+
+        for copy in copies:
+            copy.wait_send()
+        if slot == 0:
+            for other in (left, right, twin):
+                pl.semaphore_signal(done_sem, inc=1, device_id={"ep": other}, device_id_type=MESH)
+            pl.semaphore_wait(done_sem, 3)
+
+    @pl.when(pipe == 0)
+    def _():
+        hand_on(0).wait_send()
+        hand_on(1).wait_send()
+
+
+def ring_relay(first, second, gates, gain, w_gate_up, w_down):
+    tokens, width = first.shape
+    experts = lax.axis_size("ep")
     hidden_units = w_down.shape[2]
-    rows = lax.all_gather(normed, "ep", axis=0, tiled=True)
-    joined = jnp.dot(rows, w_gate_up[0, 0], preferred_element_type=jnp.float32)
-    active = (jax.nn.silu(joined[:, :hidden_units]) * joined[:, hidden_units:]).astype(jnp.bfloat16)
-    produced = jnp.dot(active, w_down[0, 0], preferred_element_type=jnp.float32)
-    scaled = (produced * gates[:, None]).astype(jnp.bfloat16)
-    summed = lax.psum_scatter(scaled, "ep", scatter_dimension=0, tiled=True)
-    return (hidden.astype(jnp.float32) + summed.astype(jnp.float32)).astype(jnp.bfloat16)
+    chips = experts // 2
+    exchanges = 4 * (chips - 1) + 3 * chips
+    kind = first.dtype
+    in_vmem = pl.BlockSpec(memory_space=pltpu.VMEM)
+    in_hbm = pl.BlockSpec(memory_space=pl.ANY)
+    return pl.pallas_call(
+        functools.partial(ring_kernel, chips),
+        out_shape=jax.ShapeDtypeStruct((2, tokens, width), kind),
+        in_specs=[in_vmem] * 4 + [in_hbm] * 2,
+        out_specs=in_vmem,
+        scratch_shapes=[
+            pltpu.VMEM((experts * tokens, width), kind),
+            pltpu.VMEM((experts * tokens, width), kind),
+            pltpu.VMEM((4 * tokens, hidden_units), kind),
+            pltpu.VMEM((chips * tokens, width), kind),
+            pltpu.VMEM((chips // 2 * tokens, width), kind),
+            pltpu.VMEM((chips // 2 * tokens, width), kind),
+            pltpu.VMEM((tokens, width), kind),
+            pltpu.VMEM(w_gate_up.shape[2:], kind),
+            pltpu.VMEM(w_down.shape[2:], kind),
+            pltpu.SemaphoreType.DMA((2,)),
+            pltpu.SemaphoreType.DMA((exchanges,)),
+            pltpu.SemaphoreType.DMA((exchanges,)),
+            pltpu.SemaphoreType.DMA((2,)),
+            pltpu.SemaphoreType.DMA((2,)),
+            pltpu.SemaphoreType.REGULAR,
+        ],
+        compiler_params=pltpu.CompilerParams(
+            collective_id=0, has_side_effects=True, vmem_limit_bytes=62_000_000
+        ),
+    )(first, second, gain, gates, w_gate_up, w_down)
 
 
 def per_device(fresh, pending, expert_ids, chosen_groups, affinity, norm_gain, w_gate_up, w_down):
     at_start = lax.axis_index("pipe") == 0
 
     tokens, experts = pending.shape[0], lax.axis_size("ep")
-    gathering = gathers_whole_blocks(tokens, experts)
-    if gathering:
+    if lax.axis_size("pipe") == 2 and gathers_whole_blocks(tokens, experts):
         columns = jnp.stack(
             [
                 gate_columns(expert_ids[0, j], chosen_groups[0, j], affinity[0, j], experts)
@@ -109,10 +385,16 @@
             ]
         )
         columns = lax.all_to_all(columns, "ep", split_axis=2, concat_axis=1, tiled=True)[:, :, 0]
+        chips = experts // 2
+        me = lax.axis_index("ep")
+        places = (ring_place(me, chips) + chips - jnp.array(ring_offsets(chips))) % chips
+        order = 2 * ring_chip(places, chips)[:, None] + jnp.stack([me % 2, 1 - me % 2])
+        columns = jnp.take(columns.reshape(2, experts, tokens), order.reshape(-1), axis=1)
+        columns = columns.reshape(2, experts * tokens, 1)
+        first = jnp.where(at_start, fresh[0], pending)
+        return ring_relay(first, fresh[1], columns, norm_gain, w_gate_up, w_down)[None, :]
 
     def run_slot(place_index, layer_in):
-        if gathering:
-            return dense_layer(layer_in, columns[place_index], norm_gain[0], w_gate_up, w_down)
         return moe_layer(
             layer_in,
             expert_ids[0, place_index],

time: 420 us -> 205 us (0.49)
  waiting for transfers between devices: 313 us -> 0.01 us
  Pallas kernels: 0 us -> 181 us
  matrix products: 66 us -> 0 us
  between operations: 13.2 us -> 0.06 us
  blocking collectives: 10.6 us -> 0 us
  local copies, waits for them, and re-layouts: 2.37 us -> 8.7 us
  starting transfers between devices: 1.42 us -> 6.52 us
    reduce_scatter x2 -> x0, waiting for transfers between devices: 181 us -> none  [dense_layer(): summed = lax.psum_scatter(scaled, 'ep', scatter_dimension=0, tiled=True)]
    pallas_call x0 -> x1, Pallas kernels: none -> 181 us  [ring_relay(): pl.pallas_call(functools.partial(ring_kernel, chips), out_shape=jax.Shape...]
    all_gather x2 -> x0, waiting for transfers between devices: 121 us -> none  [dense_layer(): rows = lax.all_gather(normed, 'ep', axis=0, tiled=True)]
    dot_general x4 -> x0, matrix products: 66 us -> none  [the longest x2 40 us: dense_layer(): joined = jnp.dot(rows, w_gate_up[0, 0], preferred_element_type=jnp.float32)]
    ppermute x1 -> x0, waiting for transfers between devices: 11.3 us -> none  [from_behind(): lax.ppermute(value, axis, [(source, source + steps) for source in range(f...]
    all_to_all x1 -> x0, blocking collectives: 10.6 us -> none  [per_device(): lax.all_to_all(columns, 'ep', split_axis=2, concat_axis=1, tiled=True)]
    all_to_all x0 -> x1, starting transfers between devices: none -> 6.52 us  [per_device(): lax.all_to_all(columns, 'ep', split_axis=2, concat_axis=1, tiled=True)]
  transfers between devices with their start and end apart: 5 -> 1, of which waited for: 5 -> 0; matrix products, arithmetic and copies ran while one was open for 1% -> 2% of each run, Pallas kernels for 0% -> 0%
where the time goes in v3:
time: 205 us; the launch traced here: 203 us
  Pallas kernels  181 us (88%)
  local copies, waits for them, and re-layouts  8.7 us (4%)
  other arithmetic  6.94 us (3%)
  starting transfers between devices  6.52 us (3%)
    pallas_call x1, Pallas kernels, ring_relay(): pl.pallas_call(functools.partial(ring_kernel, chips), out_shape=jax.Shape...  181 us
    all_to_all x1, starting transfers between devices, per_device(): lax.all_to_all(columns, 'ep', split_axis=2, concat_axis=1, tiled=True)  6.52 us
  transfers between devices with their start and end apart: 1, of which 0 were waited for; matrix products, arithmetic and copies ran while one was open for 2% of the time, Pallas kernels for 0%

profile of v3, /device:TPU:15, one launch (start us, length us, event | category | flops | bytes accessed | tf_op | source)
XLA Modules:
  0.0 202.8 jit_solution(7015067903746064120)
XLA Ops:
  0.0 0.7 add_select_fusion.1
  0.7 0.7 slice_bitcast_fusion.2
  1.4 0.7 slice_reduce_fusion.1
  2.1 0.7 slice_bitcast_fusion.4
  2.8 0.7 fusion.3
  3.6 0.7 reshape.196
  4.3 6.5 %all-to-all-start = ((f32[16,1,128]{2,1,0:T(1,128)}), f32[16,1,128]{2,1,0:T(1,128)S(1)}, u32[]{:S(2)}, u32[]{:S(2)}) async-start(f32[16,1,128]{2,1,0:T(1,128)} %reshape.196), calls=%async_computation | async-start | bytes 16384 | tf_op jit(solution)/shard_map/all_to_all | solution.py:387
  10.8 0.1 pad_add_fusion
  10.9 0.7 add_multiply_fusion
  11.6 0.1 broadcast_add_fusion
  11.7 0.1 add.95
  11.8 0.1 add.93
  11.9 1.9 slice_bitcast_fusion.second_ref
  13.7 2.0 bitcast_select_fusion.first_ref
  15.7 0.1 broadcast_in_dim.45
  15.8 0.1 broadcast_in_dim.46
  15.9 0.6 broadcast.216
  16.5 0.7 reduce.2
  17.2 0.1 reshape.197
  17.3 0.6 gather_fusion
  17.8 1.0 gather.10
  18.9 1.2 broadcast_select_fusion.gate_ref
  20.1 180.6 %shard_map.91 = bf16[2,64,3584]{2,1,0:T(8,128)(2,1)} custom-call(bf16[64,3584]{1,0:T(8,128)(2,1)} %bitcast_select_fusion.first_ref, bf16[64,3584]{1,0:T(8,128)(2,1)} %slice_bitcast_fusion.second_ref, f32[1,3584]{1,0:T(1,128)} %gain_ref.1, f32[2,1024,1]{2,1,0:T(8,128)} %broadcast_select_fusion.gate_ref, bf16[1,1,3584,2048]{3,2,1,0:T(8,128)(2,1)} %up_hbm.1, ...), custom_call_target="tpu_custom_call" | custom-call | tf_op jit(solution)/shard_map/pallas_call | solution.py:348
  200.6 2.2 %copy.31 = bf16[1,2,64,3584]{3,2,1,0:T(8,128)(2,1)} copy(bf16[1,2,64,3584]{3,2,1,0:T(8,128)(2,1)} %bitcast.42) | data formatting | bytes 1835008
  (10 shorter events, 0.1 us)
Async XLA Ops:
  4.3 11.5 %all-to-all-start = ((f32[16,1,128]{2,1,0:T(1,128)}), f32[16,1,128]{2,1,0:T(1,128)S(1)}, u32[]{:S(2)}, u32[]{:S(2)}) async-start(f32[16,1,128]{2,1,0:T(1,128)} %reshape.196), calls=%async_computation | async-start | bytes 16384 | tf_op jit(solution)/shard_map/all_to_all | solution.py:387

commit v4 on v3

--- a/solution.py
+++ b/solution.py
@@ -9,6 +9,7 @@
 
 TOP = 8
 GROUPS = 8
+LANES = 128
 
 
 EPSILON = 1e-06
@@ -78,13 +79,13 @@
 
 
 def gathers_whole_blocks(tokens, experts):
-    ring = experts % 4 == 0 and experts > 8 and tokens % 32 == 0
+    ring = experts % 4 == 0 and experts > 8 and tokens % 32 == 0 and 2 * experts <= LANES
     return ring and 2 * slot_capacity(tokens, experts) > tokens
 
 
 def gate_columns(routes, groups, affinity, experts):
     weights = gate_table(routes, groups, affinity, experts)
-    expert_iota = jnp.arange(experts, dtype=jnp.int32)
+    expert_iota = jnp.arange(LANES, dtype=jnp.int32) % experts
     hit = routes[:, :, None] == expert_iota
     return jnp.sum(jnp.where(hit, weights[:, :, None], 0.0), axis=1)
 
@@ -111,12 +112,13 @@
 
 
 def ring_kernel(
-    chips, first_ref, second_ref, gain_ref, gate_ref, up_hbm, down_hbm, out_ref,
+    chips, fresh_ref, pending_ref, gain_ref, gate_ref, up_hbm, down_hbm, out_ref,
     rows, part, act, from_twin, from_right, from_left, held, up, down,
     load_sem, send_sem, recv_sem, pipe_send_sem, pipe_recv_sem, done_sem,
 ):
-    tokens, width = first_ref.shape
+    tokens, width = pending_ref.shape
     half_rows = tokens // 2
+    experts, lanes = 2 * chips, gate_ref.shape[2]
     hidden_units = down.shape[0]
     ahead = chips // 2
     blocks = {offset: block for block, offset in enumerate(ring_offsets(chips))}
@@ -162,15 +164,19 @@
         @pl.loop(0, hidden_units // 256)
         def _(tile):
             at = pl.multiple_of(tile * 256, 256)
-            x = rows[span, :]
+            x = rows[span, pl.ds(0, width)]
             a = jnp.dot(x, up[:, pl.ds(at, 256)], preferred_element_type=jnp.float32)
             b = jnp.dot(
                 x, up[:, pl.ds(hidden_units + at, 256)], preferred_element_type=jnp.float32
             )
             act[pl.ds(0, size), pl.ds(at, 256)] = (a / (1.0 + jnp.exp(-a)) * b).astype(act.dtype)
 
-    def expert_down(slot, block, count):
+    def expert_down(block, count):
         span, size = pl.ds(2 * block * tokens, 2 * count * tokens), 2 * count * tokens
+        lane = lax.broadcasted_iota(jnp.int32, (size, lanes), 1)
+        parts = rows[span, pl.ds(width, lanes)].astype(jnp.float32)
+        ours = (lane == me) | (lane == experts + me)
+        gate = jnp.sum(jnp.where(ours, parts, 0.0), axis=1, keepdims=True)
 
         @pl.loop(0, width // 512)
         def _(tile):
@@ -179,7 +185,7 @@
                 act[pl.ds(0, size), :], down[:, pl.ds(at, 512)],
                 preferred_element_type=jnp.float32,
             )
-            part[span, pl.ds(at, 512)] = (y * gate_ref[slot, span, :]).astype(part.dtype)
+            part[span, pl.ds(at, 512)] = (y * gate).astype(part.dtype)
 
     def combine(block, half, *arrived):
         at = pl.ds(2 * block * tokens + half * half_rows, half_rows)
@@ -198,6 +204,12 @@
             device_id={"pipe": 1 - pipe},
             device_id_type=MESH,
         )
+
+    def layer_in(slot, at):
+        if slot:
+            return held[at, :].astype(jnp.float32)
+        fresh, pending = fresh_ref[0, at, :], pending_ref[at, :]
+        return jnp.where(pipe == 0, fresh.astype(jnp.float32), pending.astype(jnp.float32))
 
     for slot in range(2):
         copies = []
@@ -217,23 +229,27 @@
             return copy
 
         gathers, forwards, swaps, reduces = {}, {}, {}, {}
-        layer_in = held if slot else first_ref
         for half in range(2):
             at = pl.ds(half * half_rows, half_rows)
             if slot:
 
                 @pl.when(pipe == 0)
                 def _():
-                    held[at, :] = second_ref[at, :]
+                    held[at, :] = fresh_ref[1, at, :]
 
                 @pl.when(pipe == 1)
                 def _():
                     hand_on(half).wait_recv()
 
-            widened = layer_in[at, :].astype(jnp.float32)
+            widened = layer_in(slot, at)
             mean_square = jnp.mean(widened * widened, axis=-1, keepdims=True)
             normed = widened * lax.rsqrt(mean_square + EPSILON) * gain_ref[...]
-            rows[at, :] = normed.astype(rows.dtype)
+            rows[at, pl.ds(0, width)] = normed.astype(rows.dtype)
+            gate = gate_ref[slot, at, :]
+            high = gate.astype(rows.dtype).astype(jnp.float32)
+            lane = lax.broadcasted_iota(jnp.int32, gate.shape, 1)
+            packed = jnp.where(lane < experts, high, gate - high)
+            rows[at, pl.ds(width, lanes)] = packed.astype(rows.dtype)
             source = mine(rows, 0, half)
             for toward, other in (("right", right), ("left", left)):
                 target = mine(rows, behind_of(1, toward), half)
@@ -290,7 +306,7 @@
                 arrive(step, 1)
             if slot == 0 and step == 1:
                 load_down.wait()
-            expert_down(slot, group[0], len(group))
+            expert_down(group[0], len(group))
             for block in group:
                 swap(block)
             if step < ahead:
@@ -301,7 +317,7 @@
         for half in range(2):
             forwards[group[0], half].wait_recv()
         expert_up(group[0], 1)
-        expert_down(slot, group[0], 1)
+        expert_down(group[0], 1)
         swap(group[0])
         for step in range(ahead, 0, -1):
             reduce(step, 0, "right")
@@ -315,7 +331,7 @@
             reduces[1, half, "left"].wait_recv()
             at = pl.ds(half * half_rows, half_rows)
             total = combine(0, half, (from_left, 0), (from_right, 0))
-            result = layer_in[at, :].astype(jnp.float32) + total
+            result = layer_in(slot, at) + total
             out_ref[slot, at, :] = result.astype(out_ref.dtype)
             if slot == 0:
 
@@ -336,13 +352,13 @@
         hand_on(1).wait_send()
 
 
-def ring_relay(first, second, gates, gain, w_gate_up, w_down):
-    tokens, width = first.shape
+def ring_relay(fresh, pending, gates, gain, w_gate_up, w_down):
+    tokens, width = pending.shape
     experts = lax.axis_size("ep")
     hidden_units = w_down.shape[2]
     chips = experts // 2
     exchanges = 4 * (chips - 1) + 3 * chips
-    kind = first.dtype
+    kind = pending.dtype
     in_vmem = pl.BlockSpec(memory_space=pltpu.VMEM)
     in_hbm = pl.BlockSpec(memory_space=pl.ANY)
     return pl.pallas_call(
@@ -351,7 +367,7 @@
         in_specs=[in_vmem] * 4 + [in_hbm] * 2,
         out_specs=in_vmem,
         scratch_shapes=[
-            pltpu.VMEM((experts * tokens, width), kind),
+            pltpu.VMEM((experts * tokens, width + gates.shape[2]), kind),
             pltpu.VMEM((experts * tokens, width), kind),
             pltpu.VMEM((4 * tokens, hidden_units), kind),
             pltpu.VMEM((chips * tokens, width), kind),
@@ -370,7 +386,7 @@
         compiler_params=pltpu.CompilerParams(
             collective_id=0, has_side_effects=True, vmem_limit_bytes=62_000_000
         ),
-    )(first, second, gain, gates, w_gate_up, w_down)
+    )(fresh, pending, gain, gates, w_gate_up, w_down)
 
 
 def per_device(fresh, pending, expert_ids, chosen_groups, affinity, norm_gain, w_gate_up, w_down):
@@ -384,15 +400,7 @@
                 for j in range(2)
             ]
         )
-        columns = lax.all_to_all(columns, "ep", split_axis=2, concat_axis=1, tiled=True)[:, :, 0]
-        chips = experts // 2
-        me = lax.axis_index("ep")
-        places = (ring_place(me, chips) + chips - jnp.array(ring_offsets(chips))) % chips
-        order = 2 * ring_chip(places, chips)[:, None] + jnp.stack([me % 2, 1 - me % 2])
-        columns = jnp.take(columns.reshape(2, experts, tokens), order.reshape(-1), axis=1)
-        columns = columns.reshape(2, experts * tokens, 1)
-        first = jnp.where(at_start, fresh[0], pending)
-        return ring_relay(first, fresh[1], columns, norm_gain, w_gate_up, w_down)[None, :]
+        return ring_relay(fresh, pending, columns, norm_gain, w_gate_up, w_down)[None, :]
 
     def run_slot(place_index, layer_in):
         return moe_layer(

time: 205 us -> 193 us (0.941)
  starting transfers between devices: 6.52 us -> 0 us
  local copies, waits for them, and re-layouts: 8.7 us -> 3.9 us
  other arithmetic: 6.94 us -> 3.14 us
  Pallas kernels: 181 us -> 184 us
    all_to_all x1 -> x0, starting transfers between devices: 6.52 us -> none  [per_device(): lax.all_to_all(columns, 'ep', split_axis=2, concat_axis=1, tiled=True)]
    select_n x3 -> x1, other arithmetic: 3.17 us -> 0.01 us  [gate_columns(): expert_iota = jnp.arange(LANES, dtype=jnp.int32) % experts]
    pallas_call x1, Pallas kernels: 181 us -> 184 us  [ring_relay(): pl.pallas_call(functools.partial(ring_kernel, chips), out_shape=jax.Shape...]
  transfers between devices with their start and end apart: 1 -> 0, of which waited for: 0 -> 0; matrix products, arithmetic and copies ran while one was open for 2% -> 0% of each run, Pallas kernels for 0% -> 0%
where the time goes in v4:
time: 193 us; the launch traced here: 191 us
  Pallas kernels  184 us (95%)
  local copies, waits for them, and re-layouts  3.9 us (2%)
  other arithmetic  3.14 us (2%)
    pallas_call x1, Pallas kernels, ring_relay(): pl.pallas_call(functools.partial(ring_kernel, chips), out_shape=jax.Shape...  184 us

profile of v4, /device:TPU:15, one launch (start us, length us, event | category | flops | bytes accessed | tf_op | source)
XLA Modules:
  0.0 190.7 jit_solution(11137439170412865622)
XLA Ops:
  0.0 0.7 slice_reduce_fusion.1
  0.7 0.7 slice_bitcast_fusion.2
  1.4 0.7 slice_bitcast_fusion
  2.1 0.7 add_select_fusion
  2.9 0.7 fusion.2
  3.6 0.1 copy.20
  3.7 0.1 copy.19
  3.7 0.1 copy.18
  3.8 0.1 copy.17
  3.9 0.3 select_reduce_fusion.1
  4.3 0.6 pad_maximum_fusion.gate_ref
  4.9 183.6 %shard_map.82 = bf16[2,64,3584]{2,1,0:T(8,128)(2,1)} custom-call(bf16[2,64,3584]{2,1,0:T(8,128)(2,1)} %fresh_ref.1, bf16[64,3584]{1,0:T(8,128)(2,1)} %pending_ref.1, f32[1,3584]{1,0:T(1,128)} %gain_ref.1, f32[2,64,128]{2,1,0:T(8,128)} %pad_maximum_fusion.gate_ref, bf16[1,1,3584,2048]{3,2,1,0:T(8,128)(2,1)} %up_hbm.1, bf16[1,1,1024,3584]{3,2,1,0:T(8,128)(2,1)} %down_hbm.1), custom_call_target="tpu_custom_call" | custom-call | tf_op jit(solution)/shard_map/pallas_call | solution.py:364
  188.5 2.2 %copy.22 = bf16[1,2,64,3584]{3,2,1,0:T(8,128)(2,1)} copy(bf16[1,2,64,3584]{3,2,1,0:T(8,128)(2,1)} %bitcast.23) | data formatting | bytes 1835008
  (2 shorter events, 0.0 us)
